TPU v7x, 256 devices: a whole 4x4x8 slice. The times are simulated.
256 devices in a mesh: orb: 8 (over y, z_hi), aux: 32 (over x, z_lo, core).
Axes of the slice: x: 4, y: 4, z: 8 (z_hi: 2, z_lo: 4; z = z_hi * 4 + z_lo), core: 2. Of those that a mesh axis runs over, the one named last changes fastest.
Arguments:
- factors: bfloat16 [16, 32768, 512], P('orb', 'aux'), may hold values from -0.5 to 0.5
- occ_energy: float32 [16], replicated, may hold values from -2 to -0.5
- virt_energy: float32 [16, 512], replicated, may hold values from 0.2 to 3
- tile_table: int32 [16, 3], replicated, may hold values from 0 to 15, as said below
Outputs:
- gamma: bfloat16 [16, 32768, 512], P('orb', 'aux')
Inputs may be any that keep to these rules, and one draw needn't show every extreme that they name: Row t names two different blocks and the group tile_table[t, 2] that computes the tile. Each group computes at most 4 tiles, and some group exactly 4. Of the blocks owned by another group, the tiles of one group name at most one.
All inputs are finite; a program needn't handle non-finite values.
Results may differ from a plain program's by a relative error of at most 0.0053.
Values may be sent and summed in bfloat16 or wider, within the bound.
A program may use at most 192 MiB of HBM per device.

v0:
```python
import jax
import jax.numpy as jnp
from jax import lax
from jax.sharding import PartitionSpec as P

CAP = 4


def cut_along(array, dim, devices):
    lengths = array.shape
    pieces = array.reshape(*lengths[:dim], devices, lengths[dim] // devices, *lengths[dim + 1 :])
    return jnp.moveaxis(pieces, dim, 0)


def summed_on_arrival(array, axis, dim):
    pieces = cut_along(array, dim, lax.axis_size(axis))
    arrived = lax.all_to_all(pieces, axis, split_axis=0, concat_axis=0, tiled=True)
    return arrived.sum(axis=0)


def in_order(pieces, dim):
    lengths = list(pieces.shape[1:])
    lengths[dim] *= pieces.shape[0]
    return jnp.moveaxis(pieces, 0, dim).reshape(lengths)


def sent_to_all(array, axis):
    copies = jnp.broadcast_to(array, (lax.axis_size(axis), *array.shape))
    return lax.all_to_all(copies, axis, split_axis=0, concat_axis=0, tiled=True)


def gather_directly(array, axis, dim):
    return in_order(sent_to_all(array, axis), dim)


def settle_tile(products, denominators):
    share = summed_on_arrival(products, "aux", 0)
    rows = share.shape[0]
    start = lax.axis_index("aux") * rows
    below = lax.dynamic_slice_in_dim(denominators, start, rows, 0)
    amp_share = (share / below).astype(jnp.bfloat16)
    return gather_directly(amp_share, "aux", 0)


def shards(factors, occ_energy, virt_energy, tile_table):
    owned = factors.shape[0]
    groups = lax.axis_size("orb")
    mine = lax.axis_index("orb")
    first = tile_table[:, 0]
    second = tile_table[:, 1]
    helper = tile_table[:, 2]
    block_ids = jnp.arange(owned * groups, dtype=jnp.int32)
    group_ids = jnp.arange(groups, dtype=jnp.int32)
    local_ids = jnp.arange(owned, dtype=jnp.int32)
    touched = (
        (first[:, None] == block_ids[None, :]) | (second[:, None] == block_ids[None, :])
    ).astype(jnp.int32)
    helped = (helper[:, None] == group_ids[None, :]).astype(jnp.int32)
    usage = jnp.sum(helped[:, :, None] * touched[:, None, :], axis=0) > 0
    usage = usage.reshape(groups, groups, owned).astype(jnp.int32)
    own_usage = jnp.take(usage, mine, axis=1)
    send_pick = jnp.sum(own_usage * local_ids[None, :], axis=1)
    outgoing = jnp.take(factors, send_pick, axis=0)
    incoming = lax.all_to_all(outgoing, "orb", split_axis=0, concat_axis=0, tiled=True)
    store = jnp.concatenate([factors, incoming], axis=0)

    def position(block):
        owner = block // owned
        return jnp.where(owner == mine, block % owned, owned + owner)

    is_mine = (helper == mine).astype(jnp.int32)
    rank = jnp.cumsum(is_mine) - 1
    slot_ids = jnp.arange(CAP, dtype=jnp.int32)
    picked = is_mine[None, :] * (rank[None, :] == slot_ids[:, None]).astype(jnp.int32)
    valid = jnp.sum(picked, axis=1)
    tile_p = jnp.sum(picked * first[None, :], axis=1)
    tile_q = jnp.sum(picked * second[None, :], axis=1)
    place_p = position(tile_p)
    place_q = position(tile_q)
    energy_p = jnp.take(virt_energy, tile_p, axis=0)
    energy_q = jnp.take(virt_energy, tile_q, axis=0)
    occ_sum = jnp.take(occ_energy, tile_p) + jnp.take(occ_energy, tile_q)
    denominators = energy_p[:, :, None] + energy_q[:, None, :] - occ_sum[:, None, None]

    def partners(slot):
        block_p = lax.dynamic_index_in_dim(store, place_p[slot], 0, keepdims=False)
        block_q = lax.dynamic_index_in_dim(store, place_q[slot], 0, keepdims=False)
        return (block_p, block_q)

    def tile_products(slot):
        block_p, block_q = partners(slot)
        return lax.dot_general(
            block_p, block_q, (((0,), (0,)), ((), ())), preferred_element_type=jnp.float32
        )

    def spread(slot, amplitudes, gathered):
        block_p, block_q = partners(slot)
        amplitudes = jnp.where(valid[slot] > 0, amplitudes, jnp.zeros_like(amplitudes))
        to_first = lax.dot_general(
            block_q, amplitudes, (((1,), (1,)), ((), ())), preferred_element_type=jnp.float32
        )
        to_second = jnp.dot(block_p, amplitudes, preferred_element_type=jnp.float32)
        gathered = gathered.at[place_p[slot]].add(to_first)
        return gathered.at[place_q[slot]].add(to_second)

    gathered = jnp.zeros(store.shape, jnp.float32)

    def one_slot(slot, gathered):
        below = lax.dynamic_index_in_dim(denominators, slot, 0, keepdims=False)
        amplitudes = settle_tile(tile_products(slot), below)
        return spread(slot, amplitudes, gathered)

    gathered = lax.fori_loop(0, CAP, one_slot, gathered)
    helper_part = gathered[owned:].astype(jnp.bfloat16)
    returned = lax.all_to_all(helper_part, "orb", split_axis=0, concat_axis=0, tiled=True)
    landing = (send_pick[:, None] == local_ids[None, :]).astype(jnp.float32)
    gamma = gathered[:owned] + jnp.einsum(
        "dj,dav->jav", landing, returned.astype(jnp.float32), precision=lax.Precision.HIGHEST
    )
    return gamma.astype(jnp.bfloat16)


def solution(mesh):
    return jax.shard_map(
        shards,
        mesh=mesh,
        in_specs=(P("orb", "aux", None), P(), P(), P()),
        out_specs=P("orb", "aux", None),
        check_vma=False,
    )
```

profile of v0, /device:TPU:33, one launch (start us, length us, event | category | flops | bytes accessed | tf_op | source)
XLA Modules:
  0.0 753.1 jit_solution(9369538784813106193)
XLA Ops:
  0.0 0.8 slice_bitcast_fusion.2
  1.2 6.0 gather_fusion
  7.2 7.5 broadcast_select_fusion.1
  14.6 10.1 %all-to-all-start.2 = ((bf16[8,1024,512]{2,1,0:T(8,128)(2,1)}), bf16[8,1024,512]{2,1,0:T(8,128)(2,1)}, u32[]{:S(2)}, u32[]{:S(2)}) async-start(bf16[8,1024,512]{2,1,0:T(8,128)(2,1)} %broadcast_select_fusion.1), calls=%async_computation.2 | async-start | bytes 16777216 | tf_op jit(solution)/shard_map/all_to_all | solution.py:64
  27.8 2.4 add_subtract_fusion
  30.3 182.3 %all-to-all-done.2 = bf16[8,1024,512]{2,1,0:T(8,128)(2,1)} async-done(((bf16[8,1024,512]{2,1,0:T(8,128)(2,1)}), bf16[8,1024,512]{2,1,0:T(8,128)(2,1)}, u32[]{:S(2)}, u32[]{:S(2)}) %all-to-all-start.2) | async-done | bytes 8388640 | tf_op jit(solution)/shard_map/all_to_all | solution.py:64
  212.6 8.7 %pad_maximum_fusion = bf16[10,1024,512]{2,1,0:T(8,128)(2,1)} fusion(bf16[8,1024,512]{2,1,0:T(8,128)(2,1)} %all-to-all-done.2, bf16[2,1024,512]{2,1,0:T(8,128)(2,1)S(1)} %copy-done.3), kind=kLoop, calls=%fused_computation.30 | loop fusion | flops 5242880 | bytes 20971520 | tf_op jit(solution)/shard_map/concatenate | solution.py:65
  221.3 9.7 %broadcast_in_dim.64 = f32[10,1024,512]{2,1,0:T(8,128)} broadcast(f32[]{:T(128)} %constant.363.clone.1), dimensions={} | broadcast | bytes 20971524 | tf_op jit(solution)/shard_map/broadcast_in_dim | solution.py:106
  231.0 306.1 %while.19 = (s32[]{:T(128)}, f32[10,1024,512]{2,1,0:T(8,128)}, s32[4]{0:T(128)S(1)}, s32[4]{0:T(128)S(1)}, bf16[10,1024,512]{2,1,0:T(8,128)(2,1)}, /*index=5*/s3...) while((s32[]{:T(128)}, f32[10,1024,512]{2,1,0:T(8,128)}, ...), condition=%wide.region_10.13_spmd, body=%wide.region_6.12_spmd.sunk | while | flops 1613242368 | bytes 26349548 | solution.py:113
  232.9 0.7 dynamic_slice.101
  235.5 1.3 dynamic-slice_bitcast_fusion.2
  238.0 2.9 fusion.48
  240.9 19.0 %all-to-all-start = ((f32[32,16,512]{2,1,0:T(8,128)}), f32[32,16,512]{2,1,0:T(8,128)S(1)}, u32[]{:S(2)}, u32[]{:S(2)}) async-start(f32[32,16,512]{2,1,0:T(8,128)} %fusion.48), calls=%async_computation | async-start | bytes 2097152 | tf_op jit(solution)/shard_map/while/body/eval_jaxpr/all_to_all | solution.py:17
  260.0 24.1 %all-to-all-done = f32[32,16,512]{2,1,0:T(8,128)S(1)} async-done(((f32[32,16,512]{2,1,0:T(8,128)}), f32[32,16,512]{2,1,0:T(8,128)S(1)}, u32[]{:S(2)}, u32[]{:S(2)}) %all-to-all-start) | async-done | bytes 1048608 | tf_op jit(solution)/shard_map/while/body/eval_jaxpr/all_to_all | solution.py:17
  284.2 0.8 fusion.49
  285.0 0.9 broadcast_in_dim.84
  285.9 7.5 %all-to-all-start.1 = ((bf16[32,16,512]{2,1,0:T(8,128)(2,1)}), bf16[32,16,512]{2,1,0:T(8,128)(2,1)S(1)}, u32[]{:S(2)}, u32[]{:S(2)}) async-start(bf16[32,16,512]{2,1,0:T(8,128)(2,1)} %broadcast_in_dim.84), calls=%async_computation.1 | async-start | bytes 1048576 | tf_op jit(solution)/shard_map/while/body/eval_jaxpr/all_to_all | solution.py:29
  293.4 0.6 dynamic_slice.102
  294.8 0.8 and_reduce_fusion.3
  295.5 12.6 %all-to-all-done.1 = bf16[32,16,512]{2,1,0:T(8,128)(2,1)S(1)} async-done(((bf16[32,16,512]{2,1,0:T(8,128)(2,1)}), bf16[32,16,512]{2,1,0:T(8,128)(2,1)S(1)}, u32[]{:S(2)}, u32[]{:S(2)}) %all-to-all-start.1) | async-done | bytes 524320 | tf_op jit(solution)/shard_map/while/body/eval_jaxpr/all_to_all | solution.py:29
  308.2 4.6 fusion.50
  312.8 4.6 fusion.51
  319.3 0.7 dynamic_slice.101
  321.9 1.3 dynamic-slice_bitcast_fusion.2
  324.4 2.9 fusion.48
  327.3 5.8 all-to-all-start
  333.2 24.1 %all-to-all-done = f32[32,16,512]{2,1,0:T(8,128)S(1)} async-done(((f32[32,16,512]{2,1,0:T(8,128)}), f32[32,16,512]{2,1,0:T(8,128)S(1)}, u32[]{:S(2)}, u32[]{:S(2)}) %all-to-all-start) | async-done | bytes 1048608 | tf_op jit(solution)/shard_map/while/body/eval_jaxpr/all_to_all | solution.py:17
  357.4 0.8 fusion.49
  358.2 0.9 broadcast_in_dim.84
  359.1 7.6 %all-to-all-start.1 = ((bf16[32,16,512]{2,1,0:T(8,128)(2,1)}), bf16[32,16,512]{2,1,0:T(8,128)(2,1)S(1)}, u32[]{:S(2)}, u32[]{:S(2)}) async-start(bf16[32,16,512]{2,1,0:T(8,128)(2,1)} %broadcast_in_dim.84), calls=%async_computation.1 | async-start | bytes 1048576 | tf_op jit(solution)/shard_map/while/body/eval_jaxpr/all_to_all | solution.py:29
  368.0 0.8 and_reduce_fusion.3
  368.8 12.6 %all-to-all-done.1 = bf16[32,16,512]{2,1,0:T(8,128)(2,1)S(1)} async-done(((bf16[32,16,512]{2,1,0:T(8,128)(2,1)}), bf16[32,16,512]{2,1,0:T(8,128)(2,1)S(1)}, u32[]{:S(2)}, u32[]{:S(2)}) %all-to-all-start.1) | async-done | bytes 524320 | tf_op jit(solution)/shard_map/while/body/eval_jaxpr/all_to_all | solution.py:29
  381.4 4.6 fusion.50
  386.0 4.6 fusion.51
  392.5 0.7 dynamic_slice.101
  395.2 1.3 dynamic-slice_bitcast_fusion.2
  397.7 2.9 fusion.48
  400.6 5.8 all-to-all-start
  406.4 24.1 %all-to-all-done = f32[32,16,512]{2,1,0:T(8,128)S(1)} async-done(((f32[32,16,512]{2,1,0:T(8,128)}), f32[32,16,512]{2,1,0:T(8,128)S(1)}, u32[]{:S(2)}, u32[]{:S(2)}) %all-to-all-start) | async-done | bytes 1048608 | tf_op jit(solution)/shard_map/while/body/eval_jaxpr/all_to_all | solution.py:17
  430.6 0.8 fusion.49
  431.5 0.9 broadcast_in_dim.84
  432.3 7.6 %all-to-all-start.1 = ((bf16[32,16,512]{2,1,0:T(8,128)(2,1)}), bf16[32,16,512]{2,1,0:T(8,128)(2,1)S(1)}, u32[]{:S(2)}, u32[]{:S(2)}) async-start(bf16[32,16,512]{2,1,0:T(8,128)(2,1)} %broadcast_in_dim.84), calls=%async_computation.1 | async-start | bytes 1048576 | tf_op jit(solution)/shard_map/while/body/eval_jaxpr/all_to_all | solution.py:29
  441.2 0.8 and_reduce_fusion.3
  442.0 12.6 %all-to-all-done.1 = bf16[32,16,512]{2,1,0:T(8,128)(2,1)S(1)} async-done(((bf16[32,16,512]{2,1,0:T(8,128)(2,1)}), bf16[32,16,512]{2,1,0:T(8,128)(2,1)S(1)}, u32[]{:S(2)}, u32[]{:S(2)}) %all-to-all-start.1) | async-done | bytes 524320 | tf_op jit(solution)/shard_map/while/body/eval_jaxpr/all_to_all | solution.py:29
  454.6 4.6 fusion.50
  459.2 4.6 fusion.51
  465.7 0.7 dynamic_slice.101
  468.4 1.3 dynamic-slice_bitcast_fusion.2
  470.9 2.9 fusion.48
  473.8 5.8 all-to-all-start
  479.6 24.1 %all-to-all-done = f32[32,16,512]{2,1,0:T(8,128)S(1)} async-done(((f32[32,16,512]{2,1,0:T(8,128)}), f32[32,16,512]{2,1,0:T(8,128)S(1)}, u32[]{:S(2)}, u32[]{:S(2)}) %all-to-all-start) | async-done | bytes 1048608 | tf_op jit(solution)/shard_map/while/body/eval_jaxpr/all_to_all | solution.py:17
  503.8 0.8 fusion.49
  504.7 0.9 broadcast_in_dim.84
  505.5 7.6 %all-to-all-start.1 = ((bf16[32,16,512]{2,1,0:T(8,128)(2,1)}), bf16[32,16,512]{2,1,0:T(8,128)(2,1)S(1)}, u32[]{:S(2)}, u32[]{:S(2)}) async-start(bf16[32,16,512]{2,1,0:T(8,128)(2,1)} %broadcast_in_dim.84), calls=%async_computation.1 | async-start | bytes 1048576 | tf_op jit(solution)/shard_map/while/body/eval_jaxpr/all_to_all | solution.py:29
  514.5 0.8 and_reduce_fusion.3
  515.2 12.6 %all-to-all-done.1 = bf16[32,16,512]{2,1,0:T(8,128)(2,1)S(1)} async-done(((bf16[32,16,512]{2,1,0:T(8,128)(2,1)}), bf16[32,16,512]{2,1,0:T(8,128)(2,1)S(1)}, u32[]{:S(2)}, u32[]{:S(2)}) %all-to-all-start.1) | async-done | bytes 524320 | tf_op jit(solution)/shard_map/while/body/eval_jaxpr/all_to_all | solution.py:29
  527.9 4.6 fusion.50
  532.5 4.6 fusion.51
  537.1 9.0 %slice.122 = bf16[8,1024,512]{2,1,0:T(8,128)(2,1)} slice(f32[10,1024,512]{2,1,0:T(8,128)} %get-tuple-element.247), slice={[2:10], [0:1024], [0:512]} | slice | bytes 16777216 | tf_op jit(solution)/shard_map/slice | solution.py:114
  546.1 5.9 all-to-all-start.3
  552.0 26.1 %copy.22 = f32[10,1024,512]{2,0,1:T(8,128)} copy(f32[10,1024,512]{2,1,0:T(8,128)} %get-tuple-element.247) | data formatting | bytes 41943040 | tf_op jit(solution)/shard_map/while | solution.py:113
  578.1 161.7 %all-to-all-done.3 = bf16[8,1024,512]{2,1,0:T(8,128)(2,1)} async-done(((bf16[8,1024,512]{2,1,0:T(8,128)(2,1)}), bf16[8,1024,512]{2,1,0:T(8,128)(2,1)}, u32[]{:S(2)}, u32[]{:S(2)}) %all-to-all-start.3) | async-done | bytes 8388640 | tf_op jit(solution)/shard_map/all_to_all | solution.py:115
  739.8 11.7 %fusion.15 = bf16[2,1024,512]{2,0,1:T(2,128)(2,1)S(1)} fusion(f32[10,1024,512]{2,0,1:T(8,128)} %copy.22, bf16[8,1024,512]{2,1,0:T(8,128)(2,1)} %all-to-all-done.3, s32[8]{0:T(128)S(1)} %fusion.25), kind=kOutput, calls=%fused_computation.35 | convolution fusion | flops 18874384 | bytes 14680096 | tf_op jit(solution)/shard_map/dj,dav->jav/dot_general | solution.py:117
  751.5 1.7 copy.24
  (57 shorter events, 10.2 us)
Async XLA Ops:
  0.0 26.5 %copy-start = (f32[16,512]{1,0:T(8,128)S(1)}, f32[16,512]{1,0:T(8,128)}, u32[]{:S(2)}) copy-start(f32[16,512]{1,0:T(8,128)} %param.16) | copy-start | bytes 98308
  14.6 10.1 %copy-start.5 = (s32[16,3]{0,1:T(4,128)S(1)}, s32[16,3]{0,1:T(4,128)}, u32[]{:S(2)}) copy-start(s32[16,3]{0,1:T(4,128)} %param.17) | copy-start | bytes 580
  14.6 10.6 %copy-start.2 = (f32[16]{0:T(128)S(1)}, f32[16]{0:T(128)}, u32[]{:S(2)}) copy-start(f32[16]{0:T(128)} %param.15) | copy-start | bytes 196
  14.6 197.9 %copy-start.3 = (bf16[2,1024,512]{2,1,0:T(8,128)(2,1)S(1)}, bf16[2,1024,512]{2,1,0:T(8,128)(2,1)}, u32[]{:S(2)}) copy-start(bf16[2,1024,512]{2,1,0:T(8,128)(2,1)} %param.14) | copy-start | bytes 6291460
  14.6 197.9 %all-to-all-start.2 = ((bf16[8,1024,512]{2,1,0:T(8,128)(2,1)}), bf16[8,1024,512]{2,1,0:T(8,128)(2,1)}, u32[]{:S(2)}, u32[]{:S(2)}) async-start(bf16[8,1024,512]{2,1,0:T(8,128)(2,1)} %broadcast_select_fusion.1), calls=%async_computation.2 | async-start | bytes 16777216 | tf_op jit(solution)/shard_map/all_to_all | solution.py:64
  221.3 9.7 %copy-start.4 = (s32[3]{0:T(128)S(1)}, s32[3]{0:T(128)}, u32[]{:S(2)}) copy-start(s32[3]{0:T(128)} %constant.352.clone.1) | copy-start | bytes 40
  240.9 43.2 %all-to-all-start = ((f32[32,16,512]{2,1,0:T(8,128)}), f32[32,16,512]{2,1,0:T(8,128)S(1)}, u32[]{:S(2)}, u32[]{:S(2)}) async-start(f32[32,16,512]{2,1,0:T(8,128)} %fusion.48), calls=%async_computation | async-start | bytes 2097152 | tf_op jit(solution)/shard_map/while/body/eval_jaxpr/all_to_all | solution.py:17
  285.9 22.2 %all-to-all-start.1 = ((bf16[32,16,512]{2,1,0:T(8,128)(2,1)}), bf16[32,16,512]{2,1,0:T(8,128)(2,1)S(1)}, u32[]{:S(2)}, u32[]{:S(2)}) async-start(bf16[32,16,512]{2,1,0:T(8,128)(2,1)} %broadcast_in_dim.84), calls=%async_computation.1 | async-start | bytes 1048576 | tf_op jit(solution)/shard_map/while/body/eval_jaxpr/all_to_all | solution.py:29
  327.3 30.0 %all-to-all-start = ((f32[32,16,512]{2,1,0:T(8,128)}), f32[32,16,512]{2,1,0:T(8,128)S(1)}, u32[]{:S(2)}, u32[]{:S(2)}) async-start(f32[32,16,512]{2,1,0:T(8,128)} %fusion.48), calls=%async_computation | async-start | bytes 2097152 | tf_op jit(solution)/shard_map/while/body/eval_jaxpr/all_to_all | solution.py:17
  359.1 22.3 %all-to-all-start.1 = ((bf16[32,16,512]{2,1,0:T(8,128)(2,1)}), bf16[32,16,512]{2,1,0:T(8,128)(2,1)S(1)}, u32[]{:S(2)}, u32[]{:S(2)}) async-start(bf16[32,16,512]{2,1,0:T(8,128)(2,1)} %broadcast_in_dim.84), calls=%async_computation.1 | async-start | bytes 1048576 | tf_op jit(solution)/shard_map/while/body/eval_jaxpr/all_to_all | solution.py:29
  400.6 30.0 %all-to-all-start = ((f32[32,16,512]{2,1,0:T(8,128)}), f32[32,16,512]{2,1,0:T(8,128)S(1)}, u32[]{:S(2)}, u32[]{:S(2)}) async-start(f32[32,16,512]{2,1,0:T(8,128)} %fusion.48), calls=%async_computation | async-start | bytes 2097152 | tf_op jit(solution)/shard_map/while/body/eval_jaxpr/all_to_all | solution.py:17
  432.3 22.3 %all-to-all-start.1 = ((bf16[32,16,512]{2,1,0:T(8,128)(2,1)}), bf16[32,16,512]{2,1,0:T(8,128)(2,1)S(1)}, u32[]{:S(2)}, u32[]{:S(2)}) async-start(bf16[32,16,512]{2,1,0:T(8,128)(2,1)} %broadcast_in_dim.84), calls=%async_computation.1 | async-start | bytes 1048576 | tf_op jit(solution)/shard_map/while/body/eval_jaxpr/all_to_all | solution.py:29
  473.8 30.0 %all-to-all-start = ((f32[32,16,512]{2,1,0:T(8,128)}), f32[32,16,512]{2,1,0:T(8,128)S(1)}, u32[]{:S(2)}, u32[]{:S(2)}) async-start(f32[32,16,512]{2,1,0:T(8,128)} %fusion.48), calls=%async_computation | async-start | bytes 2097152 | tf_op jit(solution)/shard_map/while/body/eval_jaxpr/all_to_all | solution.py:17
  505.5 22.3 %all-to-all-start.1 = ((bf16[32,16,512]{2,1,0:T(8,128)(2,1)}), bf16[32,16,512]{2,1,0:T(8,128)(2,1)S(1)}, u32[]{:S(2)}, u32[]{:S(2)}) async-start(bf16[32,16,512]{2,1,0:T(8,128)(2,1)} %broadcast_in_dim.84), calls=%async_computation.1 | async-start | bytes 1048576 | tf_op jit(solution)/shard_map/while/body/eval_jaxpr/all_to_all | solution.py:29
  546.1 193.7 %all-to-all-start.3 = ((bf16[8,1024,512]{2,1,0:T(8,128)(2,1)}), bf16[8,1024,512]{2,1,0:T(8,128)(2,1)}, u32[]{:S(2)}, u32[]{:S(2)}) async-start(bf16[8,1024,512]{2,1,0:T(8,128)(2,1)} %slice.122), calls=%async_computation.3 | async-start | bytes 16777216 | tf_op jit(solution)/shard_map/all_to_all | solution.py:115
  739.8 13.3 %copy-start.1 = (f32[16,512]{1,0:T(8,128)S(1)}, f32[16,512]{1,0:T(8,128)}, u32[]{:S(2)}) copy-start(f32[16,512]{1,0:T(8,128)} %param.16) | copy-start | bytes 98308
where the time goes:
time: 761 us; the launch traced here: 753 us
  waiting for transfers between devices  491 us (65%)
  starting transfers between devices  82.9 us (11%)
  local copies, waits for them, and re-layouts  74.2 us (10%)
  matrix products  60.1 us (8%)
  other arithmetic  26.2 us (3%)
  loops' own time  18.8 us (2%)
    all_to_all x1, waiting for transfers between devices, shards(): lax.all_to_all(outgoing, 'orb', split_axis=0, concat_axis=0, tiled=True)  182 us
    all_to_all x1, waiting for transfers between devices, shards(): lax.all_to_all(helper_part, 'orb', split_axis=0, concat_axis=0, tiled=True)  162 us
    all_to_all x4, waiting for transfers between devices, summed_on_arrival(): lax.all_to_all(pieces, axis, split_axis=0, concat_axis=0, tiled=True)  96.6 us
    all_to_all x4, waiting for transfers between devices, sent_to_all(): return lax.all_to_all(copies, axis, split_axis=0, concat_axis=0, tiled=True)  50.3 us
    all_to_all x4, starting transfers between devices, summed_on_arrival(): lax.all_to_all(pieces, axis, split_axis=0, concat_axis=0, tiled=True)  36.5 us
    all_to_all x4, starting transfers between devices, sent_to_all(): return lax.all_to_all(copies, axis, split_axis=0, concat_axis=0, tiled=True)  30.4 us
    while x1, local copies, waits for them, and re-layouts, shards(): gathered = lax.fori_loop(0, CAP, one_slot, gathered)  26.1 us
    another operation x1, loops' own time, shards(): gathered = lax.fori_loop(0, CAP, one_slot, gathered)  18.8 us
  transfers between devices with their start and end apart: 10, of which 10 were waited for; matrix products, arithmetic and copies ran while one was open for 5% of the time, Pallas kernels for 0%

commit v1 on v0

v1 whole, which is shorter than its diff:
```python
import jax
import jax.numpy as jnp
from jax import lax
from jax.experimental import pallas as pl
from jax.experimental.pallas import tpu as pltpu
from jax.sharding import PartitionSpec as P


def products_kernel(table, factors, out):
    tile = pl.program_id(0)
    block_p = factors[table[tile, 0]]
    block_q = factors[table[tile, 1]]
    out[0] = lax.dot_general(
        block_p, block_q, (((0,), (0,)), ((), ())), preferred_element_type=jnp.float32
    )


def tile_products(tile_table, slices):
    blocks, rows, width = slices.shape
    tiles = tile_table.shape[0]
    return pl.pallas_call(
        products_kernel,
        out_shape=jax.ShapeDtypeStruct((tiles, width, width), jnp.float32),
        grid_spec=pltpu.PrefetchScalarGridSpec(
            num_scalar_prefetch=1,
            grid=(tiles,),
            in_specs=[pl.BlockSpec((blocks, rows, width), lambda t, table: (0, 0, 0))],
            out_specs=pl.BlockSpec((1, width, width), lambda t, table: (t, 0, 0)),
        ),
        name="products",
    )(tile_table, slices)


def spread_kernel(table, factors, amplitudes, out, acc):
    tile = pl.program_id(0)

    @pl.when(tile == 0)
    def _():
        acc[...] = jnp.zeros_like(acc)

    p = table[tile, 0]
    q = table[tile, 1]
    amp = amplitudes[0]
    acc[p] += lax.dot_general(
        factors[q], amp, (((1,), (1,)), ((), ())), preferred_element_type=jnp.float32
    )
    acc[q] += jnp.dot(factors[p], amp, preferred_element_type=jnp.float32)

    @pl.when(tile == pl.num_programs(0) - 1)
    def _():
        out[...] = acc[...].astype(out.dtype)


def spread(tile_table, slices, amplitudes):
    blocks, rows, width = slices.shape
    tiles = tile_table.shape[0]
    return pl.pallas_call(
        spread_kernel,
        out_shape=jax.ShapeDtypeStruct(slices.shape, slices.dtype),
        grid_spec=pltpu.PrefetchScalarGridSpec(
            num_scalar_prefetch=1,
            grid=(tiles,),
            in_specs=[
                pl.BlockSpec((blocks, rows, width), lambda t, table: (0, 0, 0)),
                pl.BlockSpec((1, width, width), lambda t, table: (t, 0, 0)),
            ],
            out_specs=pl.BlockSpec((blocks, rows, width), lambda t, table: (0, 0, 0)),
            scratch_shapes=[pltpu.VMEM((blocks, rows, width), jnp.float32)],
        ),
        name="spread",
    )(tile_table, slices, amplitudes)


def shards(factors, occ_energy, virt_energy, tile_table):
    tiles = tile_table.shape[0]
    width = factors.shape[-1]
    devices = lax.axis_size("orb") * lax.axis_size("aux")
    mine = lax.axis_index("orb") * lax.axis_size("aux") + lax.axis_index("aux")
    slices = lax.all_to_all(factors, "orb", split_axis=1, concat_axis=0, tiled=True)
    products = tile_products(tile_table, slices).reshape(tiles * width, width)
    share = lax.psum_scatter(products, ("orb", "aux"), scatter_dimension=0, tiled=True)
    rows = tiles * width // devices
    tile = mine * rows // width
    start = mine * rows % width
    p = tile_table[tile, 0]
    q = tile_table[tile, 1]
    energy_p = lax.dynamic_slice(virt_energy, (p, start), (1, rows))[0]
    energy_q = virt_energy[q]
    below = energy_p[:, None] + energy_q[None, :] - occ_energy[p] - occ_energy[q]
    amp_share = (share / below).astype(jnp.bfloat16)
    amplitudes = lax.all_gather(amp_share, ("orb", "aux"), axis=0, tiled=True)
    gamma = spread(tile_table, slices, amplitudes.reshape(tiles, width, width))
    return lax.all_to_all(gamma, "orb", split_axis=0, concat_axis=1, tiled=True)


def solution(mesh):
    return jax.shard_map(
        shards,
        mesh=mesh,
        in_specs=(P("orb", "aux", None), P(), P(), P()),
        out_specs=P("orb", "aux", None),
        check_vma=False,
    )
```

time: 761 us -> 1890 us (2.48)
  waiting for transfers between devices: 491 us -> 1760 us
  starting transfers between devices: 82.9 us -> 10.1 us
  local copies, waits for them, and re-layouts: 74.2 us -> 10.4 us
  matrix products: 60.1 us -> 0 us
  blocking collectives: 0 us -> 58.2 us
  Pallas kernels: 0 us -> 28.9 us
  other arithmetic: 26.2 us -> 2.79 us
    reduce_scatter x0 -> x1, waiting for transfers between devices: none -> 1290 us  [shards(): lax.psum_scatter(products, ('orb', 'aux'), scatter_dimension=0, tiled=True)]
    all_to_all x10 -> x1, waiting for transfers between devices: 491 us -> 52.1 us  [shards(): lax.all_to_all(factors, 'orb', split_axis=1, concat_axis=0, tiled=True)]
    all_gather x0 -> x1, waiting for transfers between devices: none -> 423 us  [shards(): amplitudes = lax.all_gather(amp_share, ('orb', 'aux'), axis=0, tiled=True)]
    all_to_all x10 -> x1, starting transfers between devices: 82.9 us -> 10 us  [shards(): lax.all_to_all(factors, 'orb', split_axis=1, concat_axis=0, tiled=True)]
    dot_general x13 -> x0, matrix products: 60.1 us -> none  [the longest x4 18.4 us: spread(): to_second = jnp.dot(block_p, amplitudes, preferred_element_type=jnp.float32)]
    all_to_all x0 -> x1, blocking collectives: none -> 58.2 us  [shards(): return lax.all_to_all(gamma, 'orb', split_axis=0, concat_axis=1, tiled=True)]
    pallas_call x0 -> x2, Pallas kernels: none -> 28.9 us  [the longest x1 15.6 us: spread(): pl.pallas_call(spread_kernel, out_shape=jax.ShapeDtypeStruct(slices.shape...]
    while x1 -> x0, local copies, waits for them, and re-layouts: 26.1 us -> none  [shards(): gathered = lax.fori_loop(0, CAP, one_slot, gathered)]
  transfers between devices with their start and end apart: 10 -> 3, of which waited for: 10 -> 3; matrix products, arithmetic and copies ran while one was open for 5% -> 0% of each run, Pallas kernels for 0% -> 0%
where the time goes in v1:
time: 1890 us
  waiting for transfers between devices  1760 us (93%)
  blocking collectives  58.2 us (3%)
  Pallas kernels  28.9 us (2%)
    reduce_scatter x1, waiting for transfers between devices, shards(): lax.psum_scatter(products, ('orb', 'aux'), scatter_dimension=0, tiled=True)  1290 us
    all_gather x1, waiting for transfers between devices, shards(): amplitudes = lax.all_gather(amp_share, ('orb', 'aux'), axis=0, tiled=True)  423 us
    all_to_all x1, blocking collectives, shards(): return lax.all_to_all(gamma, 'orb', split_axis=0, concat_axis=1, tiled=True)  58.2 us
    all_to_all x1, waiting for transfers between devices, shards(): lax.all_to_all(factors, 'orb', split_axis=1, concat_axis=0, tiled=True)  52.1 us
  transfers between devices with their start and end apart: 3, of which 3 were waited for; matrix products, arithmetic and copies ran while one was open for 0% of the time, Pallas kernels for 0%

profile of v1, /device:TPU:33, one launch (start us, length us, event | category | flops | bytes accessed | tf_op | source)
XLA Modules:
  0.0 1890.2 jit_solution(2182719207466387080)
XLA Ops:
  6.5 0.0 copy-start
  6.5 5.1 copy.9
  11.6 0.0 copy-start.1
  11.6 10.0 all-to-all-start
  21.7 0.0 reduce-scatter.2.cloned.1.call-start
  21.7 0.0 copy-done.1
  21.7 0.7 copy.12.table
  22.4 52.1 %all-to-all-done = bf16[2,1024,512]{2,0,1:T(2,128)(2,1)S(1)} async-done(((bf16[2,1024,512]{2,0,1:T(2,128)(2,1)}), bf16[2,1024,512]{2,0,1:T(2,128)(2,1)S(1)}, u32[]{:S(2)}, u32[]{:S(2)}) %all-to-all-start) | async-done | bytes 2097184 | tf_op jit(solution)/shard_map/all_to_all | solution.py:79
  74.5 1.7 copy.10
  76.3 13.3 products.1
  89.5 0.0 copy-start.2
  89.5 0.0 reduce-scatter.2.cloned.1.call-update
  89.6 0.0 all-gather.2.cloned.1.call-start
  89.6 0.7 constant_dynamic-slice_fusion.1
  94.1 0.0 copy-done.2
  94.1 0.7 fusion
  94.7 0.0 copy-done
  94.7 0.1 dynamic-slice_bitcast_fusion
  94.8 1287.5 %reduce-scatter.2.cloned.1.call-done = f32[32,512]{1,0:T(8,128)} async-done(((f32[8192,512]{1,0:T(8,128)}), f32[32,512]{1,0:T(8,128)}) %reduce-scatter.2.cloned.1.call-update) | async-done | bytes 65552 | tf_op jit(solution)/shard_map/reduce_scatter | solution.py:81
  1382.3 2.8 divide_convert_fusion
  1385.1 0.0 all-gather.2.cloned.1.call-update
  1385.1 422.9 %all-gather.2.cloned.1.call-done = bf16[8192,512]{1,0:T(8,128)(2,1)} async-done(((bf16[32,512]{1,0:T(8,128)(2,1)}), bf16[8192,512]{1,0:T(8,128)(2,1)}) %all-gather.2.cloned.1.call-update) | async-done | bytes 8388624 | tf_op jit(solution)/shard_map/all_gather | solution.py:91
  1808.0 15.6 spread.1
  1823.6 58.2 %all_to_all.36 = bf16[16,128,512]{2,1,0:T(8,128)(2,1)S(1)} all-to-all(bf16[16,128,512]{2,1,0:T(8,128)(2,1)} %spread.1), channel_id=1, replica_groups=mesh['orb'=8,'aux'=32] {'orb'}, dimensions={0} | all-to-all | bytes 4194304 | tf_op jit(solution)/shard_map/all_to_all | solution.py:93
  1881.8 1.5 copy.13
  (1 shorter events, 0.0 us)
Async XLA Ops:
  6.5 88.2 %copy-start = (f32[16,512]{1,0:T(8,128)S(1)}, f32[16,512]{1,0:T(8,128)}, u32[]{:S(2)}) copy-start(f32[16,512]{1,0:T(8,128)} %param.6) | copy-start | bytes 98308
  11.6 10.1 copy-start.1
  11.6 62.9 %all-to-all-start = ((bf16[2,1024,512]{2,0,1:T(2,128)(2,1)}), bf16[2,1024,512]{2,0,1:T(2,128)(2,1)S(1)}, u32[]{:S(2)}, u32[]{:S(2)}) async-start(bf16[2,1024,512]{2,0,1:T(2,128)(2,1)} %copy.9), calls=%async_computation | async-start | bytes 4194304 | tf_op jit(solution)/shard_map/all_to_all | solution.py:79
  21.7 1360.6 %reduce-scatter.2.cloned.1.call-start = ((), (), s32[]{:S(2)}) async-start(), calls=%async_computation.3 | async-start | bytes 16842752 | tf_op jit(solution)/shard_map/reduce_scatter | solution.py:81
  89.5 4.5 copy-start.2
  89.6 1718.5 %all-gather.2.cloned.1.call-start = ((), (), s32[]{:S(2)}) async-start(), calls=%async_computation.4 | async-start | bytes 8421376 | tf_op jit(solution)/shard_map/all_gather | solution.py:91
Sparse Core Ops, SparseCore 0:
  89.7 1292.5 reduce-scatter.1
  1385.2 422.7 all-gather.1

commit v2 on v1

v2 whole, which is shorter than its diff:
```python
import functools

import jax
import jax.numpy as jnp
from jax import lax
from jax.experimental import pallas as pl
from jax.experimental.pallas import tpu as pltpu
from jax.sharding import PartitionSpec as P

MESH = pl.DeviceIdType.MESH
STREAMS = 4
STEPS = 4
Z = 8
CORES = 2


def place():
    orb = lax.axis_index("orb")
    aux = lax.axis_index("aux")
    return dict(
        x=aux // 8, y=orb // 2, z=(orb % 2) * 4 + (aux // 2) % 4, core=aux % 2
    )


def device(x, y, z, core):
    return {"orb": y * 2 + z // 4, "aux": x * 8 + (z % 4) * 2 + core}


def partner(at, dim):
    x, y = at["x"], at["y"]
    near_x, far_x = x + 1 - 2 * (x % 2), 3 - x
    near_y, far_y = y + 1 - 2 * (y % 2), 3 - y
    if isinstance(dim, int):
        to_x = (near_x, x, far_x, x)[dim]
        to_y = (y, near_y, y, far_y)[dim]
    else:
        to_x = jnp.where(dim == 0, near_x, jnp.where(dim == 2, far_x, x))
        to_y = jnp.where(dim == 1, near_y, jnp.where(dim == 3, far_y, y))
    return device(to_x, to_y, at["z"], at["core"])


def bits_of(at):
    return (
        ((at["x"] + 1) // 2) % 2,
        ((at["y"] + 1) // 2) % 2,
        at["x"] // 2,
        at["y"] // 2,
    )


def offsets_of(bits, rows):
    table = []
    for stream in range(STREAMS):
        kept = [0]
        for step in range(STEPS):
            half = rows >> (step + 1)
            kept.append(kept[-1] + half * bits[(stream + step) % STREAMS])
        table.append(kept)
    return table


def settle_kernel(
    table, slices, below, out,
    both, send_0, send_1, send_2, send_3, recv_0, recv_1, recv_2, recv_3,
    total, z_total, z_recv, amps,
    swap_sem, rs_send, rs_recv, z_send, z_arrive, zg_send, zg_arrive,
    ag_send, ag_recv, out_send, out_recv, out_sem,
):
    at = place()
    core, z = at["core"], at["z"]
    bits = bits_of(at)
    blocks, rows, width = slices.shape
    per_core = amps.shape[0]
    stream_rows = per_core // STREAMS
    kept = offsets_of(bits, stream_rows)
    sends = (send_0, send_1, send_2, send_3)
    recvs = (recv_0, recv_1, recv_2, recv_3)
    other_core = device(at["x"], at["y"], z, 1 - core)
    last = stream_rows >> STEPS
    z_rows = last * STREAMS // Z

    def z_peer(distance):
        return (z + distance) % Z

    barrier = pltpu.get_barrier_semaphore()
    peers = [other_core]
    peers += [partner(at, dim) for dim in range(STREAMS)]
    peers += [device(at["x"], at["y"], z_peer(d), core) for d in range(1, Z)]
    for peer in peers:
        pl.semaphore_signal(barrier, inc=1, device_id=peer, device_id_type=MESH)
    pl.semaphore_wait(barrier, len(peers))

    def remote(src, dst, send_sem, recv_sem, to):
        return pltpu.make_async_remote_copy(
            src_ref=src, dst_ref=dst, send_sem=send_sem, recv_sem=recv_sem,
            device_id=to, device_id_type=MESH,
        )

    mine = both.at[:, pl.ds(pl.multiple_of(core * rows, rows), rows), :]
    theirs = both.at[:, pl.ds(pl.multiple_of((1 - core) * rows, rows), rows), :]
    swap = remote(slices, mine, swap_sem.at[0], swap_sem.at[1], other_core)
    swap.start()
    own = pltpu.make_async_copy(slices, mine, swap_sem.at[2])
    own.start()
    own.wait()
    remote(slices, theirs, swap_sem.at[0], swap_sem.at[1], other_core).wait_recv()

    tiles = per_core // width

    def product(tile):
        block_p = both[table[core * tiles + tile, 0]]
        block_q = both[table[core * tiles + tile, 1]]
        return lax.dot_general(
            block_p, block_q, (((0,), (0,)), ((), ())), preferred_element_type=jnp.float32
        )

    def bit_at(dim):
        value = bits[3]
        for index in (2, 1, 0):
            value = jnp.where(dim == index, bits[index], value)
        return value

    def first_send(stream, carry):
        send_0[stream] = product(2 * stream + 1 - bit_at(stream)).astype(send_0.dtype)
        remote(
            send_0.at[stream], recv_0.at[stream],
            rs_send.at[0, stream], rs_recv.at[0, stream], partner(at, stream),
        ).start()
        return carry

    lax.fori_loop(0, STREAMS, first_send, 0)

    def first_keep(stream, carry):
        total[stream] = product(2 * stream + bit_at(stream))
        return carry

    lax.fori_loop(0, STREAMS, first_keep, 0)

    def rs_copy(step, stream):
        return remote(
            sends[step].at[stream], recvs[step].at[stream],
            rs_send.at[step, stream], rs_recv.at[step, stream],
            partner(at, (stream + step) % STREAMS),
        )

    for step in range(1, STEPS):
        half = stream_rows >> (step + 1)
        for stream in range(STREAMS):
            bit = bits[(stream + step) % STREAMS]
            rs_copy(step - 1, stream).wait_recv()
            base = kept[stream][step] - kept[stream][1]
            away = pl.multiple_of(base + half * (1 - bit), half)
            sends[step][stream] = (
                total[stream, pl.ds(away, half), :]
                + recvs[step - 1][stream, pl.ds(pl.multiple_of(half * (1 - bit), half), half), :]
            ).astype(send_0.dtype)
            rs_copy(step, stream).start()
        for stream in range(STREAMS):
            bit = bits[(stream + step) % STREAMS]
            base = kept[stream][step] - kept[stream][1]
            stay = pl.multiple_of(base + half * bit, half)
            total[stream, pl.ds(stay, half), :] += recvs[step - 1][
                stream, pl.ds(pl.multiple_of(half * bit, half), half), :
            ].astype(jnp.float32)

    for stream in range(STREAMS):
        rs_copy(STEPS - 1, stream).wait_recv()
        base = pl.multiple_of(kept[stream][STEPS] - kept[stream][1], last)
        z_total[pl.ds(stream * last, last), :] = (
            total[stream, pl.ds(base, last), :] + recvs[STEPS - 1][stream].astype(jnp.float32)
        )

    def z_copy(distance):
        to = z_peer(distance)
        return remote(
            z_total.at[pl.ds(pl.multiple_of(to * z_rows, z_rows), z_rows), :],
            z_recv.at[distance - 1],
            z_send.at[distance - 1], z_arrive.at[distance - 1],
            device(at["x"], at["y"], to, core),
        )

    for distance in range(1, Z):
        z_copy(distance).start()
    share = z_total[pl.ds(pl.multiple_of(z * z_rows, z_rows), z_rows), :]
    for distance in range(1, Z):
        z_copy(distance).wait_recv()
        share = share + z_recv[distance - 1]

    def settled(height):
        stream = height // (Z // STREAMS)
        start = kept[0][STEPS]
        for index in range(1, STREAMS):
            start = jnp.where(
                stream == index, index * stream_rows + kept[index][STEPS], start
            )
        return amps.at[
            pl.ds(pl.multiple_of(start + (height % (Z // STREAMS)) * z_rows, z_rows), z_rows), :
        ]

    settled(z)[...] = (share / below[...]).astype(amps.dtype)

    def zg_copy(distance, source, to):
        return remote(
            settled(source), settled(source),
            zg_send.at[distance - 1], zg_arrive.at[distance - 1],
            device(at["x"], at["y"], to, core),
        )

    for distance in range(1, Z):
        zg_copy(distance, z, z_peer(distance)).start()
    for distance in range(1, Z):
        zg_copy(distance, z_peer(Z - distance), z_peer(Z - distance)).wait_recv()

    def ag_rows(step, stream, arriving):
        size = stream_rows >> (step + 1)
        bit = bits[(stream + step) % STREAMS]
        if arriving:
            bit = 1 - bit
        start = stream * stream_rows + kept[stream][step] + size * bit
        return pl.ds(pl.multiple_of(start, size), size)

    def ag_copy(step, stream, arriving):
        piece = amps.at[ag_rows(step, stream, arriving), :]
        return remote(
            piece, piece, ag_send.at[step, stream], ag_recv.at[step, stream],
            partner(at, (stream + step) % STREAMS),
        )

    def out_copies(index, stream, arriving):
        slot = index * STREAMS + stream
        rows_here = ag_rows(0, stream, arriving)
        start = ag_rows(0, stream, arriving).start
        size = stream_rows // 2
        piece = amps.at[rows_here, :]
        here = out.at[pl.ds(pl.multiple_of(core * per_core + start, size), size), :]
        there = out.at[pl.ds(pl.multiple_of((1 - core) * per_core + start, size), size), :]
        across = remote(piece, here, out_send.at[slot], out_recv.at[slot], other_core)
        from_other = remote(piece, there, out_send.at[slot], out_recv.at[slot], other_core)
        return across, pltpu.make_async_copy(piece, here, out_sem.at[slot]), from_other

    for step in range(STEPS - 1, -1, -1):
        for stream in range(STREAMS):
            if step < STEPS - 1:
                ag_copy(step + 1, stream, True).wait_recv()
            ag_copy(step, stream, False).start()
    for stream in range(STREAMS):
        across, local, _ = out_copies(0, stream, False)
        across.start()
        local.start()
    for stream in range(STREAMS):
        ag_copy(0, stream, True).wait_recv()
        across, local, _ = out_copies(1, stream, True)
        across.start()
        local.start()

    swap.wait_send()
    for step in range(STEPS):
        for stream in range(STREAMS):
            rs_copy(step, stream).wait_send()
            ag_copy(step, stream, False).wait_send()
    for distance in range(1, Z):
        z_copy(distance).wait_send()
        zg_copy(distance, z, z_peer(distance)).wait_send()
    for index in range(2):
        for stream in range(STREAMS):
            across, local, from_other = out_copies(index, stream, index == 1)
            across.wait_send()
            from_other.wait_recv()
            local.wait()


def settle(tile_table, slices, below):
    blocks, rows, width = slices.shape
    tiles = tile_table.shape[0]
    per_core = tiles * width // CORES
    stream_rows = per_core // STREAMS
    halves = [stream_rows >> (step + 1) for step in range(STEPS)]
    wire = [pltpu.VMEM((STREAMS, half, width), jnp.bfloat16) for half in halves]
    last = halves[-1] * STREAMS
    dma = pltpu.SemaphoreType.DMA
    return pl.pallas_call(
        settle_kernel,
        out_shape=jax.ShapeDtypeStruct((tiles * width, width), jnp.bfloat16),
        in_specs=[
            pl.BlockSpec(memory_space=pltpu.SMEM),
            pl.BlockSpec(memory_space=pl.ANY),
            pl.BlockSpec(memory_space=pltpu.VMEM),
        ],
        out_specs=pl.BlockSpec(memory_space=pl.ANY),
        scratch_shapes=[
            pltpu.VMEM((blocks, CORES * rows, width), jnp.bfloat16),
            *wire,
            *wire,
            pltpu.VMEM((STREAMS, halves[0], width), jnp.float32),
            pltpu.VMEM((last, width), jnp.float32),
            pltpu.VMEM((Z - 1, last // Z, width), jnp.float32),
            pltpu.VMEM((per_core, width), jnp.bfloat16),
            dma((3,)),
            dma((STEPS, STREAMS)),
            dma((STEPS, STREAMS)),
            dma((Z - 1,)),
            dma((Z - 1,)),
            dma((Z - 1,)),
            dma((Z - 1,)),
            dma((STEPS, STREAMS)),
            dma((STEPS, STREAMS)),
            dma((2 * STREAMS,)),
            dma((2 * STREAMS,)),
            dma((2 * STREAMS,)),
        ],
        compiler_params=pltpu.CompilerParams(
            collective_id=0, has_side_effects=True, vmem_limit_bytes=48 << 20
        ),
        name="settle",
    )(tile_table, slices, below)


def settled_place(tiles, width):
    at = place()
    bits = bits_of(at)
    per_core = tiles * width // CORES
    stream_rows = per_core // STREAMS
    kept = offsets_of(bits, stream_rows)
    stream = at["z"] // (Z // STREAMS)
    rows = (stream_rows >> STEPS) * STREAMS // Z
    start = kept[0][STEPS]
    for index in range(1, STREAMS):
        start = jnp.where(stream == index, kept[index][STEPS], start)
    start = (
        at["core"] * per_core
        + stream * stream_rows
        + start
        + (at["z"] % (Z // STREAMS)) * rows
    )
    return start // width, start % width, rows


def spread_kernel(table, factors, amplitudes, out, acc):
    tile = pl.program_id(0)

    @pl.when(tile == 0)
    def _():
        acc[...] = jnp.zeros_like(acc)

    p = table[tile, 0]
    q = table[tile, 1]
    amp = amplitudes[0]
    acc[p] += lax.dot_general(
        factors[q], amp, (((1,), (1,)), ((), ())), preferred_element_type=jnp.float32
    )
    acc[q] += jnp.dot(factors[p], amp, preferred_element_type=jnp.float32)

    @pl.when(tile == pl.num_programs(0) - 1)
    def _():
        out[...] = acc[...].astype(out.dtype)


def spread(tile_table, slices, amplitudes):
    blocks, rows, width = slices.shape
    tiles = tile_table.shape[0]
    return pl.pallas_call(
        spread_kernel,
        out_shape=jax.ShapeDtypeStruct(slices.shape, slices.dtype),
        grid_spec=pltpu.PrefetchScalarGridSpec(
            num_scalar_prefetch=1,
            grid=(tiles,),
            in_specs=[
                pl.BlockSpec((blocks, rows, width), lambda t, table: (0, 0, 0)),
                pl.BlockSpec((1, width, width), lambda t, table: (t, 0, 0)),
            ],
            out_specs=pl.BlockSpec((blocks, rows, width), lambda t, table: (0, 0, 0)),
            scratch_shapes=[pltpu.VMEM((blocks, rows, width), jnp.float32)],
        ),
        name="spread",
    )(tile_table, slices, amplitudes)


def shards(factors, occ_energy, virt_energy, tile_table):
    tiles = tile_table.shape[0]
    width = factors.shape[-1]
    slices = lax.all_to_all(factors, "orb", split_axis=1, concat_axis=0, tiled=True)
    tile, start, rows = settled_place(tiles, width)
    p = tile_table[tile, 0]
    q = tile_table[tile, 1]
    energy_p = lax.dynamic_slice(virt_energy, (p, start), (1, rows))[0]
    energy_q = virt_energy[q]
    below = energy_p[:, None] + energy_q[None, :] - occ_energy[p] - occ_energy[q]
    amplitudes = settle(tile_table, slices, below)
    gamma = spread(tile_table, slices, amplitudes.reshape(tiles, width, width))
    return lax.all_to_all(gamma, "orb", split_axis=0, concat_axis=1, tiled=True)


def solution(mesh):
    return jax.shard_map(
        shards,
        mesh=mesh,
        in_specs=(P("orb", "aux", None), P(), P(), P()),
        out_specs=P("orb", "aux", None),
        check_vma=False,
    )
```

time: 1890 us -> 237 us (0.13)
  waiting for transfers between devices: 1760 us -> 46 us
  Pallas kernels: 28.9 us -> 106 us
    reduce_scatter x1 -> x0, waiting for transfers between devices: 1290 us -> none  [shards(): lax.psum_scatter(products, ('orb', 'aux'), scatter_dimension=0, tiled=True)]
    all_gather x1 -> x0, waiting for transfers between devices: 423 us -> none  [shards(): amplitudes = lax.all_gather(amp_share, ('orb', 'aux'), axis=0, tiled=True)]
    pallas_call x1, Pallas kernels: 13.3 us -> 90.2 us  [settle(): pl.pallas_call(settle_kernel, out_shape=jax.ShapeDtypeStruct((tiles * wid...]
  transfers between devices with their start and end apart: 3 -> 1, of which waited for: 3 -> 1; matrix products, arithmetic and copies ran while one was open for 0% -> 1% of each run, Pallas kernels for 0% -> 0%
where the time goes in v2:
time: 237 us; the launch traced here: 235 us
  Pallas kernels  106 us (45%)
  blocking collectives  59.6 us (25%)
  waiting for transfers between devices  46 us (19%)
  starting transfers between devices  10 us (4%)
  local copies, waits for them, and re-layouts  8.49 us (4%)
  between operations  4 us (2%)
    pallas_call x1, Pallas kernels, settle(): pl.pallas_call(settle_kernel, out_shape=jax.ShapeDtypeStruct((tiles * wid...  90.2 us
    all_to_all x1, blocking collectives, shards(): return lax.all_to_all(gamma, 'orb', split_axis=0, concat_axis=1, tiled=True)  59.6 us
    all_to_all x1, waiting for transfers between devices, shards(): lax.all_to_all(factors, 'orb', split_axis=1, concat_axis=0, tiled=True)  46 us
    pallas_call x1, Pallas kernels, spread(): pl.pallas_call(spread_kernel, out_shape=jax.ShapeDtypeStruct(slices.shape...  15.6 us
    all_to_all x1, starting transfers between devices, shards(): lax.all_to_all(factors, 'orb', split_axis=1, concat_axis=0, tiled=True)  10 us
    unnamed x12, local copies, waits for them, and re-layouts  5.18 us
  transfers between devices with their start and end apart: 1, of which 1 were waited for; matrix products, arithmetic and copies ran while one was open for 1% of the time, Pallas kernels for 0%

profile of v2, /device:TPU:33, one launch (start us, length us, event | category | flops | bytes accessed | tf_op | source)
XLA Modules:
  0.0 235.4 jit_solution(9863535796311082104)
XLA Ops:
  0.0 0.0 copy-start
  0.0 5.1 %copy.9 = bf16[2,1024,512]{2,0,1:T(2,128)(2,1)} copy(bf16[2,1024,512]{2,1,0:T(8,128)(2,1)} %param.4) | data formatting | bytes 4194304 | tf_op args[0]
  5.1 0.0 copy-start.3
  5.1 0.0 copy-start.4
  5.1 10.0 %all-to-all-start = ((bf16[2,1024,512]{2,0,1:T(2,128)(2,1)}), bf16[2,1024,512]{2,0,1:T(2,128)(2,1)S(1)}, u32[]{:S(2)}, u32[]{:S(2)}) async-start(bf16[2,1024,512]{2,0,1:T(2,128)(2,1)} %copy.9), calls=%async_computation | async-start | bytes 4194304 | tf_op jit(solution)/shard_map/all_to_all | solution.py:381
  15.1 0.0 copy-done.3
  15.1 0.7 constant_dynamic-slice_fusion.1
  18.4 0.1 copy.12.table
  18.5 0.0 copy-start.2
  19.8 0.0 copy-done.4
  19.8 0.7 fusion
  20.5 0.0 copy-done
  20.5 0.1 dynamic-slice_bitcast_fusion
  20.6 1.4 subtract_subtract_fusion.below
  22.0 46.0 %all-to-all-done = bf16[2,1024,512]{2,0,1:T(2,128)(2,1)S(1)} async-done(((bf16[2,1024,512]{2,0,1:T(2,128)(2,1)}), bf16[2,1024,512]{2,0,1:T(2,128)(2,1)S(1)}, u32[]{:S(2)}, u32[]{:S(2)}) %all-to-all-start) | async-done | bytes 2097184 | tf_op jit(solution)/shard_map/all_to_all | solution.py:381
  68.0 0.4 copy.10
  68.4 0.0 copy-start.1
  68.4 0.0 copy-done.2
  68.4 90.2 %settle.1 = bf16[8192,512]{1,0:T(8,128)(2,1)} custom-call(s32[16,3]{1,0:T(8,128)S(1)} %copy.12.table, bf16[16,128,512]{2,1,0:T(8,128)(2,1)S(1)} %bitcast.16, f32[32,512]{1,0:T(8,128)S(1)} %subtract_subtract_fusion.below), custom_call_target="tpu_custom_call" | custom-call | tf_op jit(solution)/shard_map/settle/pallas_call | solution.py:281
  158.7 0.0 copy-done.1
  158.7 15.6 %spread.1 = bf16[16,128,512]{2,1,0:T(8,128)(2,1)} custom-call(s32[16,3]{1,0:T(8,128)} %copy-done.2, bf16[16,128,512]{2,1,0:T(8,128)(2,1)} %bitcast.17, bf16[16,512,512]{2,1,0:T(8,128)(2,1)} %bitcast.18), custom_call_target="tpu_custom_call" | custom-call | tf_op jit(solution)/shard_map/spread/pallas_call | solution.py:361
  174.3 59.6 %all_to_all.36 = bf16[16,128,512]{2,1,0:T(8,128)(2,1)S(1)} all-to-all(bf16[16,128,512]{2,1,0:T(8,128)(2,1)} %spread.1), channel_id=1, replica_groups=mesh['orb'=8,'aux'=32] {'orb'}, dimensions={0} | all-to-all | bytes 4194304 | tf_op jit(solution)/shard_map/all_to_all | solution.py:390
  233.9 1.5 copy.13
  (1 shorter events, 0.0 us)
Async XLA Ops:
  0.0 20.5 %copy-start = (f32[16,512]{1,0:T(8,128)S(1)}, f32[16,512]{1,0:T(8,128)}, u32[]{:S(2)}) copy-start(f32[16,512]{1,0:T(8,128)} %param.6) | copy-start | bytes 98308
  5.1 10.1 %copy-start.3 = (s32[16,3]{0,1:T(4,128)S(1)}, s32[16,3]{0,1:T(4,128)}, u32[]{:S(2)}) copy-start(s32[16,3]{0,1:T(4,128)} %param.7) | copy-start | bytes 580
  5.1 14.7 %copy-start.4 = (f32[16]{0:T(128)S(1)}, f32[16]{0:T(128)}, u32[]{:S(2)}) copy-start(f32[16]{0:T(128)} %param.5) | copy-start | bytes 196
  5.1 62.9 %all-to-all-start = ((bf16[2,1024,512]{2,0,1:T(2,128)(2,1)}), bf16[2,1024,512]{2,0,1:T(2,128)(2,1)S(1)}, u32[]{:S(2)}, u32[]{:S(2)}) async-start(bf16[2,1024,512]{2,0,1:T(2,128)(2,1)} %copy.9), calls=%async_computation | async-start | bytes 4194304 | tf_op jit(solution)/shard_map/all_to_all | solution.py:381
  18.5 49.9 %copy-start.2 = (s32[16,3]{1,0:T(8,128)}, s32[16,3]{1,0:T(8,128)S(1)}, u32[]{:S(2)}) copy-start(s32[16,3]{1,0:T(8,128)S(1)} %copy.12.table) | copy-start | bytes 580
  68.4 90.3 %copy-start.1 = (bf16[2,8,128,512]{3,2,0,1:T(8,128)(2,1)}, bf16[2,8,128,512]{3,2,0,1:T(8,128)(2,1)S(1)}, u32[]{:S(2)}) copy-start(bf16[2,8,128,512]{3,2,0,1:T(8,128)(2,1)S(1)} %copy.10) | copy-start | bytes 6291460

commit v3 on v1

v3 whole, which is shorter than its diff:
```python
import jax
import jax.numpy as jnp
from jax import lax
from jax.experimental import pallas as pl
from jax.experimental.pallas import tpu as pltpu
from jax.sharding import PartitionSpec as P

MESH = pl.DeviceIdType.MESH
STREAMS = 4
STEPS = 4
PARTS = 2
Z = 8
CORES = 2
ORB = 8
FAR_FIRST = (3, 5, 1, 7, 4, 2, 6)
NEAR_FIRST = (2, 6, 4, 1, 7, 3, 5)


def device(x, y, z, core):
    return {"orb": y * 2 + z // 4, "aux": x * 8 + (z % 4) * 2 + core}


def pick(options, index):
    if isinstance(index, int):
        return options[index]
    value = options[-1]
    for position in range(len(options) - 2, -1, -1):
        value = jnp.where(index == position, options[position], value)
    return value


def rows_at(start, size):
    return pl.ds(pl.multiple_of(start, size), size)


def kernel(
    table, occ, factors, virt, out,
    both, send_0, send_1, send_2, send_3, recv_0, recv_1, recv_2, recv_3,
    total, z_total, z_recv, amps, sums, gamma,
    in_send, in_recv, swap_send, swap_recv, rs_send, rs_recv, z_send, z_arrive,
    zg_send, zg_arrive, ag_send, ag_recv, cross_send, cross_recv, back_send, back_recv, local_sem,
):
    orb = lax.axis_index("orb")
    aux = lax.axis_index("aux")
    x, y, core = aux // 8, orb // 2, aux % 2
    z = (orb % 2) * 4 + (aux // 2) % 4
    near_x, far_x = x + 1 - 2 * (x % 2), 3 - x
    near_y, far_y = y + 1 - 2 * (y % 2), 3 - y
    bits = (((x + 1) // 2) % 2, ((y + 1) // 2) % 2, x // 2, y // 2)
    across_x = (near_x, x, far_x, x)
    across_y = (y, near_y, y, far_y)
    other_core = device(x, y, z, 1 - core)

    sends = (send_0, send_1, send_2, send_3)
    recvs = (recv_0, recv_1, recv_2, recv_3)
    owned, shard_rows, width = factors.shape
    blocks = both.shape[1]
    rows = shard_rows // ORB
    tiles = table.shape[0]
    per_core = amps.shape[1] // CORES
    core_tiles = tiles // CORES
    stream_rows = per_core // STREAMS
    last = stream_rows >> STEPS
    z_rows = last * STREAMS // Z
    columns = width // PARTS
    kept = []
    for stream in range(STREAMS):
        starts = [0]
        for step in range(STEPS):
            starts.append(
                starts[-1] + (stream_rows >> (step + 1)) * bits[(stream + step) % STREAMS]
            )
        kept.append(starts)

    def partner(dim):
        return device(pick(across_x, dim), pick(across_y, dim), z, core)

    def orb_peer(distance):
        return (orb + distance) % ORB

    def z_peer(distance):
        return (z + distance) % Z

    def z_device(height):
        return device(x, y, height, core)

    def remote(src, dst, send_sem, recv_sem, to):
        return pltpu.make_async_remote_copy(
            src_ref=src, dst_ref=dst, send_sem=send_sem, recv_sem=recv_sem,
            device_id=to, device_id_type=MESH,
        )

    barrier = pltpu.get_barrier_semaphore()
    peers = [other_core, partner(0), partner(2)]
    peers += [{"orb": orb_peer(d), "aux": aux} for d in range(1, ORB)]
    peers += [z_device(z_peer(d)) for d in range(1, Z) if d != Z // 2]
    for peer in peers:
        pl.semaphore_signal(barrier, inc=1, device_id=peer, device_id_type=MESH)
    pl.semaphore_wait(barrier, len(peers))

    def slices_of(source, which_core):
        return both.at[which_core, rows_at(source * owned, owned)]

    def in_copies(distance, source):
        to = orb_peer(distance)
        return [
            remote(
                factors.at[block, rows_at(to * rows, rows), :],
                both.at[core, source * owned + block],
                in_send.at[distance - 1, block], in_recv.at[distance - 1, block],
                {"orb": to, "aux": aux},
            )
            for block in range(owned)
        ]

    def swap_copy(distance, which_core):
        source = orb_peer(ORB - distance)
        piece = slices_of(source, which_core)
        return remote(piece, piece, swap_send.at[distance], swap_recv.at[distance], other_core)

    own_in = [
        pltpu.make_async_copy(
            factors.at[block, rows_at(orb * rows, rows), :],
            both.at[core, orb * owned + block],
            local_sem.at[0, block],
        )
        for block in range(owned)
    ]
    for distance in FAR_FIRST:
        for copy in in_copies(distance, orb):
            copy.start()
    for copy in own_in:
        copy.start()

    def tile_at(position):
        group, stream = position // STREAMS, position % STREAMS
        which_core = pick((core, 1 - core, core, 1 - core), group)
        bit = pick(bits, stream)
        bit = pick((bit, bit, 1 - bit, 1 - bit), group)
        return which_core * core_tiles + 2 * stream + bit

    dest = [table[tile_at(term // 2), term % 2] for term in range(2 * tiles)]

    def slot_of(block, before):
        slot = jnp.int32(0)
        for term in range(before):
            slot = jnp.where(dest[term] == block, term + 1, slot)
        return slot

    prev = [slot_of(dest[term], term) for term in range(2 * tiles)]
    final = [
        [slot_of(orb_peer(distance) * owned + block, 2 * tiles) for block in range(owned)]
        for distance in range(ORB)
    ]
    sums[0] = jnp.zeros(sums.shape[1:], sums.dtype)

    settle_stream = z // (Z // STREAMS)
    settle_start = settle_stream * stream_rows + (z % (Z // STREAMS)) * z_rows
    settle_start += pick([starts[STEPS] for starts in kept], settle_stream)
    settle_tile = core * core_tiles + settle_start // width
    first, second = table[settle_tile, 0], table[settle_tile, 1]
    lanes = lax.broadcasted_iota(jnp.int32, (z_rows, width), 1)
    wanted = lax.broadcasted_iota(jnp.int32, (z_rows, width), 0) + settle_start % width
    row_p = jnp.broadcast_to(virt[pl.ds(first, 1), :], (z_rows, width))
    energy_p = jnp.sum(jnp.where(lanes == wanted, row_p, 0.0), axis=1, keepdims=True)
    below = energy_p + virt[pl.ds(second, 1), :] - occ[first] - occ[second]

    for copy in own_in:
        copy.wait()
    swap_copy(0, core).start()
    for distance in NEAR_FIRST:
        for copy in in_copies(distance, orb_peer(ORB - distance)):
            copy.wait_recv()
        swap_copy(distance, core).start()
    for distance in range(ORB):
        swap_copy(distance, 1 - core).wait_recv()

    def product(tile, part):
        block_p = both[:, table[core * core_tiles + tile, 0]]
        block_q = both[
            :, table[core * core_tiles + tile, 1], :, rows_at(part * columns, columns)
        ]
        return lax.dot_general(
            block_p.reshape(CORES * rows, width),
            block_q.reshape(CORES * rows, columns),
            (((0,), (0,)), ((), ())),
            preferred_element_type=jnp.float32,
        )

    def first_send(slot, carry):
        part, stream = slot // STREAMS, slot % STREAMS
        send_0[slot] = product(2 * stream + 1 - pick(bits, stream), part).astype(send_0.dtype)
        remote(
            send_0.at[slot], recv_0.at[slot],
            rs_send.at[0, slot], rs_recv.at[0, slot], partner(stream),
        ).start()
        return carry

    lax.fori_loop(0, PARTS * STREAMS, first_send, 0)

    def first_keep(slot, carry):
        part, stream = slot // STREAMS, slot % STREAMS
        total[slot] = product(2 * stream + pick(bits, stream), part)
        return carry

    lax.fori_loop(0, PARTS * STREAMS, first_keep, 0)

    def rs_copy(step, slot):
        return remote(
            sends[step].at[slot], recvs[step].at[slot],
            rs_send.at[step, slot], rs_recv.at[step, slot],
            partner((slot % STREAMS + step) % STREAMS),
        )

    for step in range(1, STEPS):
        half = stream_rows >> (step + 1)
        for part in range(PARTS):
            slots = range(part * STREAMS, (part + 1) * STREAMS)
            for slot in slots:
                stream = slot % STREAMS
                bit = bits[(stream + step) % STREAMS]
                base = kept[stream][step] - kept[stream][1]
                rs_copy(step - 1, slot).wait_recv()
                sends[step][slot] = (
                    total[slot, rows_at(base + half * (1 - bit), half), :]
                    + recvs[step - 1][slot, rows_at(half * (1 - bit), half), :]
                ).astype(sends[step].dtype)
                rs_copy(step, slot).start()
            for slot in slots:
                stream = slot % STREAMS
                bit = bits[(stream + step) % STREAMS]
                base = kept[stream][step] - kept[stream][1]
                total[slot, rows_at(base + half * bit, half), :] += recvs[step - 1][
                    slot, rows_at(half * bit, half), :
                ].astype(jnp.float32)

    def z_copy(part, distance):
        to = z_peer(distance)
        return remote(
            z_total.at[part, rows_at(to * z_rows, z_rows), :],
            z_recv.at[part, distance - 1],
            z_send.at[part, distance - 1], z_arrive.at[part, distance - 1], z_device(to),
        )

    for part in range(PARTS):
        for stream in range(STREAMS):
            slot = part * STREAMS + stream
            rs_copy(STEPS - 1, slot).wait_recv()
            base = kept[stream][STEPS] - kept[stream][1]
            z_total[part, pl.ds(stream * last, last), :] = total[
                slot, rows_at(base, last), :
            ] + recvs[STEPS - 1][slot].astype(jnp.float32)
        for distance in range(1, Z):
            z_copy(part, distance).start()

    def settled(part, height):
        stream = height // (Z // STREAMS)
        start = core * per_core + stream * stream_rows + (height % (Z // STREAMS)) * z_rows
        start += pick([starts[STEPS] for starts in kept], stream)
        return amps.at[part, rows_at(start, z_rows), :]

    def zg_copy(part, distance, source, to):
        return remote(
            settled(part, source), settled(part, source),
            zg_send.at[part, distance - 1], zg_arrive.at[part, distance - 1], z_device(to),
        )

    for part in range(PARTS):
        share = z_total[part, rows_at(z * z_rows, z_rows), :]
        for distance in range(1, Z):
            z_copy(part, distance).wait_recv()
            share = share + z_recv[part, distance - 1]
        settled(part, z)[...] = (
            share / below[:, part * columns : (part + 1) * columns]
        ).astype(amps.dtype)
        for distance in range(1, Z):
            zg_copy(part, distance, z, z_peer(distance)).start()

    def ag_piece(step, slot, arriving):
        part, stream = slot // STREAMS, slot % STREAMS
        size = stream_rows >> (step + 1)
        bit = bits[(stream + step) % STREAMS]
        bit = 1 - bit if arriving else bit
        start = core * per_core + stream * stream_rows + kept[stream][step] + size * bit
        return amps.at[part, rows_at(start, size), :]

    def ag_copy(step, slot, arriving=False):
        piece = ag_piece(step, slot, arriving)
        return remote(
            piece, piece, ag_send.at[step, slot], ag_recv.at[step, slot],
            partner((slot % STREAMS + step) % STREAMS),
        )

    def cross_copy(late, slot, which_core):
        part, stream = slot // STREAMS, slot % STREAMS
        bit = 1 - bits[stream] if late else bits[stream]
        start = which_core * per_core + stream * stream_rows + width * bit
        piece = amps.at[part, rows_at(start, width), :]
        return remote(
            piece, piece, cross_send.at[late, slot], cross_recv.at[late, slot], other_core
        )

    for step in range(STEPS - 1, -1, -1):
        for part in range(PARTS):
            if step == STEPS - 1:
                for distance in range(1, Z):
                    source = z_peer(Z - distance)
                    zg_copy(part, distance, source, source).wait_recv()
            for stream in range(STREAMS):
                slot = part * STREAMS + stream
                if step < STEPS - 1:
                    ag_copy(step + 1, slot, True).wait_recv()
                ag_copy(step, slot).start()
                if step == 0:
                    cross_copy(0, slot, core).start()

    def terms(position):
        tile = tile_at(position)
        amp = [amps[part, rows_at(tile * width, width), :] for part in range(PARTS)]
        block_p = both[core, table[tile, 0]]
        block_q = both[core, table[tile, 1]]
        to_first = sums[prev[2 * position]]
        for part in range(PARTS):
            to_first = to_first + lax.dot_general(
                block_q[:, part * columns : (part + 1) * columns],
                amp[part],
                (((1,), (1,)), ((), ())),
                preferred_element_type=jnp.float32,
            )
        sums[2 * position + 1] = to_first
        to_second = [
            jnp.dot(block_p, amp[part], preferred_element_type=jnp.float32)
            for part in range(PARTS)
        ]
        sums[2 * position + 2] = sums[prev[2 * position + 1]] + jnp.concatenate(to_second, axis=1)

    def many_terms(group):
        for stream in range(STREAMS):
            terms(group * STREAMS + stream)

    slots = range(PARTS * STREAMS)
    many_terms(0)
    for slot in slots:
        cross_copy(0, slot, 1 - core).wait_recv()
    many_terms(1)
    for slot in slots:
        ag_copy(0, slot, True).wait_recv()
        cross_copy(1, slot, core).start()
    many_terms(2)
    for slot in slots:
        cross_copy(1, slot, 1 - core).wait_recv()
    many_terms(3)

    def back_copies(distance, source):
        to = orb_peer(distance)
        return [
            remote(
                gamma.at[distance, block], out.at[block, rows_at(source * rows, rows), :],
                back_send.at[distance - 1, block], back_recv.at[distance - 1, block],
                {"orb": to, "aux": aux},
            )
            for block in range(owned)
        ]

    def finish(distance):
        for block in range(owned):
            gamma[distance, block] = sums[final[distance][block]].astype(
                gamma.dtype
            )

    for distance in FAR_FIRST:
        finish(distance)
        for copy in back_copies(distance, orb):
            copy.start()
    finish(0)
    own_out = [
        pltpu.make_async_copy(
            gamma.at[0, block], out.at[block, rows_at(orb * rows, rows), :], local_sem.at[1, block]
        )
        for block in range(owned)
    ]
    for copy in own_out:
        copy.start()

    for distance in range(ORB):
        swap_copy(distance, core).wait_send()
    for distance in range(1, ORB):
        for copy in in_copies(distance, orb):
            copy.wait_send()
    for slot in slots:
        for step in range(STEPS):
            rs_copy(step, slot).wait_send()
            ag_copy(step, slot).wait_send()
        for late in range(2):
            cross_copy(late, slot, core).wait_send()
    for part in range(PARTS):
        for distance in range(1, Z):
            z_copy(part, distance).wait_send()
            zg_copy(part, distance, z, z_peer(distance)).wait_send()
    for distance in range(1, ORB):
        for copy in back_copies(distance, orb):
            copy.wait_send()
        for copy in back_copies(distance, orb_peer(ORB - distance)):
            copy.wait_recv()
    for copy in own_out:
        copy.wait()


def shards(factors, occ_energy, virt_energy, tile_table):
    owned, shard_rows, width = factors.shape
    blocks = owned * ORB
    rows = shard_rows // ORB
    tiles = tile_table.shape[0]
    stream_rows = tiles * width // CORES // STREAMS
    columns = width // PARTS
    slots = PARTS * STREAMS
    halves = [stream_rows >> (step + 1) for step in range(STEPS)]
    last = halves[-1] * STREAMS
    wire = [pltpu.VMEM((slots, half, columns), jnp.bfloat16) for half in halves]
    dma = pltpu.SemaphoreType.DMA
    return pl.pallas_call(
        kernel,
        out_shape=jax.ShapeDtypeStruct(factors.shape, factors.dtype),
        in_specs=[
            pl.BlockSpec(memory_space=pltpu.SMEM),
            pl.BlockSpec(memory_space=pltpu.SMEM),
            pl.BlockSpec(memory_space=pl.ANY),
            pl.BlockSpec(memory_space=pltpu.VMEM),
        ],
        out_specs=pl.BlockSpec(memory_space=pl.ANY),
        scratch_shapes=[
            pltpu.VMEM((CORES, blocks, rows, width), jnp.bfloat16),
            *wire,
            *wire,
            pltpu.VMEM((slots, halves[0], columns), jnp.float32),
            pltpu.VMEM((PARTS, last, columns), jnp.float32),
            pltpu.VMEM((PARTS, Z - 1, last // Z, columns), jnp.float32),
            pltpu.VMEM((PARTS, tiles * width, columns), jnp.bfloat16),
            pltpu.VMEM((2 * tiles + 1, rows, width), jnp.float32),
            pltpu.VMEM((ORB, owned, rows, width), jnp.bfloat16),
            dma((ORB - 1, owned)),
            dma((ORB - 1, owned)),
            dma((ORB,)),
            dma((ORB,)),
            dma((STEPS, slots)),
            dma((STEPS, slots)),
            dma((PARTS, Z - 1)),
            dma((PARTS, Z - 1)),
            dma((PARTS, Z - 1)),
            dma((PARTS, Z - 1)),
            dma((STEPS, slots)),
            dma((STEPS, slots)),
            dma((2, slots)),
            dma((2, slots)),
            dma((ORB - 1, owned)),
            dma((ORB - 1, owned)),
            dma((2, owned)),
        ],
        compiler_params=pltpu.CompilerParams(
            collective_id=0, has_side_effects=True, vmem_limit_bytes=56 << 20
        ),
        name="window",
    )(tile_table, occ_energy, factors, virt_energy)


def solution(mesh):
    return jax.shard_map(
        shards,
        mesh=mesh,
        in_specs=(P("orb", "aux", None), P(), P(), P()),
        out_specs=P("orb", "aux", None),
        check_vma=False,
    )
```

time: 1890 us -> 192 us (0.10)
  waiting for transfers between devices: 1760 us -> 0 us
  Pallas kernels: 28.9 us -> 188 us
  blocking collectives: 58.2 us -> 0 us
    reduce_scatter x1 -> x0, waiting for transfers between devices: 1290 us -> none  [shards(): lax.psum_scatter(products, ('orb', 'aux'), scatter_dimension=0, tiled=True)]
    all_gather x1 -> x0, waiting for transfers between devices: 423 us -> none  [shards(): amplitudes = lax.all_gather(amp_share, ('orb', 'aux'), axis=0, tiled=True)]
    pallas_call x2 -> x1, Pallas kernels: 28.9 us -> 188 us  [shards(): pl.pallas_call(kernel, out_shape=jax.ShapeDtypeStruct(factors.shape, fact...]
    all_to_all x1 -> x0, blocking collectives: 58.2 us -> none  [shards(): return lax.all_to_all(gamma, 'orb', split_axis=0, concat_axis=1, tiled=True)]
    all_to_all x1 -> x0, waiting for transfers between devices: 52.1 us -> none  [shards(): lax.all_to_all(factors, 'orb', split_axis=1, concat_axis=0, tiled=True)]
  transfers between devices with their start and end apart: 3 -> 0, of which waited for: 3 -> 0; matrix products, arithmetic and copies ran while one was open for 0% -> 0% of each run, Pallas kernels for 0% -> 0%
where the time goes in v3:
time: 192 us
  Pallas kernels  188 us (98%)
  local copies, waits for them, and re-layouts  4.4 us (2%)
    pallas_call x1, Pallas kernels, shards(): pl.pallas_call(kernel, out_shape=jax.ShapeDtypeStruct(factors.shape, fact...  188 us
    unnamed x2, local copies, waits for them, and re-layouts  4.4 us

profile of v3, /device:TPU:33, one launch (start us, length us, event | category | flops | bytes accessed | tf_op | source)
XLA Modules:
  0.0 191.9 jit_solution(11742471911791380222)
XLA Ops:
  0.0 1.4 copy.5.table
  1.4 187.5 %window.1 = bf16[2,1024,512]{2,1,0:T(8,128)(2,1)} custom-call(s32[16,3]{1,0:T(8,128)} %copy.5.table, f32[16]{0:T(128)} %occ.1, bf16[2,1024,512]{2,1,0:T(8,128)(2,1)} %factors.1, f32[16,512]{1,0:T(8,128)} %virt.1), custom_call_target="tpu_custom_call" | custom-call | tf_op jit(solution)/shard_map/window/pallas_call | solution.py:421
  188.9 3.0 %copy.7 = bf16[2,1024,512]{2,1,0:T(8,128)(2,1)} copy(bf16[2,1024,512]{2,1,0:T(8,128)(2,1)} %window.1) | data formatting | bytes 4194304

commit v4 on v3

--- a/solution.py
+++ b/solution.py
@@ -8,11 +8,19 @@
 MESH = pl.DeviceIdType.MESH
 STREAMS = 4
 STEPS = 4
-PARTS = 2
+PARTS = 4
+PAIR = 2
+STAGE_TIME = {
+    "keep": 0.5, "halve1": 5.0, "halve2": 8.0, "halve3": 10.5, "z": 12.5, "settle": 19.0,
+    "gather3": 24.5, "gather2": 26.5, "gather1": 29.0, "gather0": 32.0,
+}
+PART_DELAY = 0.3
+WIRE = (jnp.bfloat16, jnp.bfloat16, jnp.bfloat16, jnp.float32)
 Z = 8
 CORES = 2
 ORB = 8
 FAR_FIRST = (3, 5, 1, 7, 4, 2, 6)
+Z_FAR_FIRST = (4, 3, 5, 2, 6, 1, 7)
 NEAR_FIRST = (2, 6, 4, 1, 7, 3, 5)
 
 
@@ -36,7 +44,7 @@
 def kernel(
     table, occ, factors, virt, out,
     both, send_0, send_1, send_2, send_3, recv_0, recv_1, recv_2, recv_3,
-    total, z_total, z_recv, amps, sums, gamma,
+    total, z_total, z_wire, z_recv, amps, sums, gamma,
     in_send, in_recv, swap_send, swap_recv, rs_send, rs_recv, z_send, z_arrive,
     zg_send, zg_arrive, ag_send, ag_recv, cross_send, cross_recv, back_send, back_recv, local_sem,
 ):
@@ -175,35 +183,41 @@
     for distance in range(ORB):
         swap_copy(distance, 1 - core).wait_recv()
 
-    def product(tile, part):
+    def product(tile, pair):
         block_p = both[:, table[core * core_tiles + tile, 0]]
         block_q = both[
-            :, table[core * core_tiles + tile, 1], :, rows_at(part * columns, columns)
+            :, table[core * core_tiles + tile, 1], :, pl.ds(pair * PAIR * columns, PAIR * columns)
         ]
         return lax.dot_general(
             block_p.reshape(CORES * rows, width),
-            block_q.reshape(CORES * rows, columns),
+            block_q.reshape(CORES * rows, PAIR * columns),
             (((0,), (0,)), ((), ())),
             preferred_element_type=jnp.float32,
         )
 
-    def first_send(slot, carry):
-        part, stream = slot // STREAMS, slot % STREAMS
-        send_0[slot] = product(2 * stream + 1 - pick(bits, stream), part).astype(send_0.dtype)
-        remote(
-            send_0.at[slot], recv_0.at[slot],
-            rs_send.at[0, slot], rs_recv.at[0, slot], partner(stream),
-        ).start()
-        return carry
-
-    lax.fori_loop(0, PARTS * STREAMS, first_send, 0)
-
-    def first_keep(slot, carry):
-        part, stream = slot // STREAMS, slot % STREAMS
-        total[slot] = product(2 * stream + pick(bits, stream), part)
-        return carry
-
-    lax.fori_loop(0, PARTS * STREAMS, first_keep, 0)
+    def first_sends(pair):
+        def body(stream, carry):
+            away = product(2 * stream + 1 - pick(bits, stream), pair).astype(send_0.dtype)
+            for member in range(PAIR):
+                slot = (pair * PAIR + member) * STREAMS + stream
+                send_0[slot] = away[:, member * columns : (member + 1) * columns]
+                remote(
+                    send_0.at[slot], recv_0.at[slot],
+                    rs_send.at[0, slot], rs_recv.at[0, slot], partner(stream),
+                ).start()
+            return carry
+
+        lax.fori_loop(0, STREAMS, body, 0)
+
+    def first_keeps(pair):
+        def body(stream, carry):
+            stay = product(2 * stream + pick(bits, stream), pair)
+            for member in range(PAIR):
+                slot = (pair * PAIR + member) * STREAMS + stream
+                total[slot] = stay[:, member * columns : (member + 1) * columns]
+            return carry
+
+        lax.fori_loop(0, STREAMS, body, 0)
 
     def rs_copy(step, slot):
         return remote(
@@ -212,45 +226,46 @@
             partner((slot % STREAMS + step) % STREAMS),
         )
 
-    for step in range(1, STEPS):
+    def slots_of(part):
+        return range(part * STREAMS, (part + 1) * STREAMS)
+
+    def halve(part, step):
         half = stream_rows >> (step + 1)
-        for part in range(PARTS):
-            slots = range(part * STREAMS, (part + 1) * STREAMS)
-            for slot in slots:
-                stream = slot % STREAMS
-                bit = bits[(stream + step) % STREAMS]
-                base = kept[stream][step] - kept[stream][1]
-                rs_copy(step - 1, slot).wait_recv()
-                sends[step][slot] = (
-                    total[slot, rows_at(base + half * (1 - bit), half), :]
-                    + recvs[step - 1][slot, rows_at(half * (1 - bit), half), :]
-                ).astype(sends[step].dtype)
-                rs_copy(step, slot).start()
-            for slot in slots:
-                stream = slot % STREAMS
-                bit = bits[(stream + step) % STREAMS]
-                base = kept[stream][step] - kept[stream][1]
-                total[slot, rows_at(base + half * bit, half), :] += recvs[step - 1][
-                    slot, rows_at(half * bit, half), :
-                ].astype(jnp.float32)
+        for slot in slots_of(part):
+            stream = slot % STREAMS
+            bit = bits[(stream + step) % STREAMS]
+            base = kept[stream][step] - kept[stream][1]
+            rs_copy(step - 1, slot).wait_recv()
+            sends[step][slot] = (
+                total[slot, rows_at(base + half * (1 - bit), half), :]
+                + recvs[step - 1][slot, rows_at(half * (1 - bit), half), :]
+            ).astype(sends[step].dtype)
+            rs_copy(step, slot).start()
+        for slot in slots_of(part):
+            stream = slot % STREAMS
+            bit = bits[(stream + step) % STREAMS]
+            base = kept[stream][step] - kept[stream][1]
+            total[slot, rows_at(base + half * bit, half), :] += recvs[step - 1][
+                slot, rows_at(half * bit, half), :
+            ].astype(jnp.float32)
 
     def z_copy(part, distance):
         to = z_peer(distance)
         return remote(
-            z_total.at[part, rows_at(to * z_rows, z_rows), :],
+            z_wire.at[part, rows_at(to * z_rows, z_rows), :],
             z_recv.at[part, distance - 1],
             z_send.at[part, distance - 1], z_arrive.at[part, distance - 1], z_device(to),
         )
 
-    for part in range(PARTS):
+    def along_z(part):
         for stream in range(STREAMS):
             slot = part * STREAMS + stream
             rs_copy(STEPS - 1, slot).wait_recv()
             base = kept[stream][STEPS] - kept[stream][1]
-            z_total[part, pl.ds(stream * last, last), :] = total[
-                slot, rows_at(base, last), :
-            ] + recvs[STEPS - 1][slot].astype(jnp.float32)
-        for distance in range(1, Z):
+            summed = total[slot, rows_at(base, last), :] + recvs[STEPS - 1][slot]
+            z_total[part, pl.ds(stream * last, last), :] = summed
+            z_wire[part, pl.ds(stream * last, last), :] = summed.astype(z_wire.dtype)
+        for distance in Z_FAR_FIRST:
             z_copy(part, distance).start()
 
     def settled(part, height):
@@ -265,15 +280,15 @@
             zg_send.at[part, distance - 1], zg_arrive.at[part, distance - 1], z_device(to),
         )
 
-    for part in range(PARTS):
+    def divide(part):
         share = z_total[part, rows_at(z * z_rows, z_rows), :]
         for distance in range(1, Z):
             z_copy(part, distance).wait_recv()
-            share = share + z_recv[part, distance - 1]
+            share = share + z_recv[part, distance - 1].astype(jnp.float32)
         settled(part, z)[...] = (
             share / below[:, part * columns : (part + 1) * columns]
         ).astype(amps.dtype)
-        for distance in range(1, Z):
+        for distance in Z_FAR_FIRST:
             zg_copy(part, distance, z, z_peer(distance)).start()
 
     def ag_piece(step, slot, arriving):
@@ -300,39 +315,55 @@
             piece, piece, cross_send.at[late, slot], cross_recv.at[late, slot], other_core
         )
 
-    for step in range(STEPS - 1, -1, -1):
-        for part in range(PARTS):
-            if step == STEPS - 1:
-                for distance in range(1, Z):
-                    source = z_peer(Z - distance)
-                    zg_copy(part, distance, source, source).wait_recv()
-            for stream in range(STREAMS):
-                slot = part * STREAMS + stream
-                if step < STEPS - 1:
-                    ag_copy(step + 1, slot, True).wait_recv()
-                ag_copy(step, slot).start()
-                if step == 0:
-                    cross_copy(0, slot, core).start()
+    def gather(part, step):
+        if step == STEPS - 1:
+            for distance in range(1, Z):
+                source = z_peer(Z - distance)
+                zg_copy(part, distance, source, source).wait_recv()
+        for slot in slots_of(part):
+            if step < STEPS - 1:
+                ag_copy(step + 1, slot, True).wait_recv()
+            ag_copy(step, slot).start()
+        if step == 0:
+            for slot in slots_of(part):
+                cross_copy(0, slot, core).start()
+
+    stages = {
+        "halve1": lambda part: halve(part, 1),
+        "halve2": lambda part: halve(part, 2),
+        "halve3": lambda part: halve(part, 3),
+        "z": along_z,
+        "settle": divide,
+        "gather3": lambda part: gather(part, 3),
+        "gather2": lambda part: gather(part, 2),
+        "gather1": lambda part: gather(part, 1),
+        "gather0": lambda part: gather(part, 0),
+    }
+    wave = [
+        (STAGE_TIME[stage] + part * PART_DELAY, order, part, stages[stage])
+        for order, stage in enumerate(stages)
+        for part in range(PARTS)
+    ]
+    for pair in range(PARTS // PAIR):
+        start = pair * PAIR * PART_DELAY
+        wave.append((start, -2, pair, first_sends))
+        wave.append((start + STAGE_TIME["keep"], -1, pair, first_keeps))
+    for _, _, which, stage in sorted(wave, key=lambda entry: entry[:3]):
+        stage(which)
 
     def terms(position):
         tile = tile_at(position)
-        amp = [amps[part, rows_at(tile * width, width), :] for part in range(PARTS)]
+        amp = jnp.concatenate(
+            [amps[part, rows_at(tile * width, width), :] for part in range(PARTS)], axis=1
+        )
         block_p = both[core, table[tile, 0]]
         block_q = both[core, table[tile, 1]]
-        to_first = sums[prev[2 * position]]
-        for part in range(PARTS):
-            to_first = to_first + lax.dot_general(
-                block_q[:, part * columns : (part + 1) * columns],
-                amp[part],
-                (((1,), (1,)), ((), ())),
-                preferred_element_type=jnp.float32,
-            )
-        sums[2 * position + 1] = to_first
-        to_second = [
-            jnp.dot(block_p, amp[part], preferred_element_type=jnp.float32)
-            for part in range(PARTS)
-        ]
-        sums[2 * position + 2] = sums[prev[2 * position + 1]] + jnp.concatenate(to_second, axis=1)
+        to_first = lax.dot_general(
+            block_q, amp, (((1,), (1,)), ((), ())), preferred_element_type=jnp.float32
+        )
+        sums[2 * position + 1] = sums[prev[2 * position]] + to_first
+        to_second = jnp.dot(block_p, amp, preferred_element_type=jnp.float32)
+        sums[2 * position + 2] = sums[prev[2 * position + 1]] + to_second
 
     def many_terms(group):
         for stream in range(STREAMS):
@@ -416,7 +447,9 @@
     slots = PARTS * STREAMS
     halves = [stream_rows >> (step + 1) for step in range(STEPS)]
     last = halves[-1] * STREAMS
-    wire = [pltpu.VMEM((slots, half, columns), jnp.bfloat16) for half in halves]
+    wire = [
+        pltpu.VMEM((slots, half, columns), WIRE[step]) for step, half in enumerate(halves)
+    ]
     dma = pltpu.SemaphoreType.DMA
     return pl.pallas_call(
         kernel,
@@ -434,7 +467,8 @@
             *wire,
             pltpu.VMEM((slots, halves[0], columns), jnp.float32),
             pltpu.VMEM((PARTS, last, columns), jnp.float32),
-            pltpu.VMEM((PARTS, Z - 1, last // Z, columns), jnp.float32),
+            pltpu.VMEM((PARTS, last, columns), jnp.bfloat16),
+            pltpu.VMEM((PARTS, Z - 1, last // Z, columns), jnp.bfloat16),
             pltpu.VMEM((PARTS, tiles * width, columns), jnp.bfloat16),
             pltpu.VMEM((2 * tiles + 1, rows, width), jnp.float32),
             pltpu.VMEM((ORB, owned, rows, width), jnp.bfloat16),

time: 192 us -> 185 us (0.964)
  Pallas kernels: 188 us -> 180 us
    pallas_call x1, Pallas kernels: 188 us -> 180 us  [shards(): pl.pallas_call(kernel, out_shape=jax.ShapeDtypeStruct(factors.shape, fact...]
where the time goes in v4:
time: 185 us; the launch traced here: 184 us
  Pallas kernels  180 us (97%)
  local copies, waits for them, and re-layouts  4.4 us (2%)
    pallas_call x1, Pallas kernels, shards(): pl.pallas_call(kernel, out_shape=jax.ShapeDtypeStruct(factors.shape, fact...  180 us
    unnamed x2, local copies, waits for them, and re-layouts  4.4 us

profile of v4, /device:TPU:33, one launch (start us, length us, event | category | flops | bytes accessed | tf_op | source)
XLA Modules:
  0.0 184.4 jit_solution(13056318168920957822)
XLA Ops:
  0.0 1.4 copy.5.table
  1.4 180.0 %window.1 = bf16[2,1024,512]{2,1,0:T(8,128)(2,1)} custom-call(s32[16,3]{1,0:T(8,128)} %copy.5.table, f32[16]{0:T(128)} %occ.1, bf16[2,1024,512]{2,1,0:T(8,128)(2,1)} %factors.1, f32[16,512]{1,0:T(8,128)} %virt.1), custom_call_target="tpu_custom_call" | custom-call | tf_op jit(solution)/shard_map/window/pallas_call | solution.py:454
  181.3 3.0 %copy.7 = bf16[2,1024,512]{2,1,0:T(8,128)(2,1)} copy(bf16[2,1024,512]{2,1,0:T(8,128)(2,1)} %window.1) | data formatting | bytes 4194304

commit v5 on v4

--- a/solution.py
+++ b/solution.py
@@ -21,7 +21,7 @@
 ORB = 8
 FAR_FIRST = (3, 5, 1, 7, 4, 2, 6)
 Z_FAR_FIRST = (4, 3, 5, 2, 6, 1, 7)
-NEAR_FIRST = (2, 6, 4, 1, 7, 3, 5)
+ARRIVAL = (3, 5, 4, 2, 6, 1, 7)
 
 
 def device(x, y, z, core):
@@ -176,7 +176,7 @@
     for copy in own_in:
         copy.wait()
     swap_copy(0, core).start()
-    for distance in NEAR_FIRST:
+    for distance in ARRIVAL:
         for copy in in_copies(distance, orb_peer(ORB - distance)):
             copy.wait_recv()
         swap_copy(distance, core).start()

time: 185 us -> 184 us (level)
  no operation moved by 1% of the time
where the time goes in v5:
time: 184 us; the launch traced here: 183 us
  Pallas kernels  179 us (97%)
  local copies, waits for them, and re-layouts  4.4 us (2%)
    pallas_call x1, Pallas kernels, shards(): pl.pallas_call(kernel, out_shape=jax.ShapeDtypeStruct(factors.shape, fact...  179 us
    unnamed x2, local copies, waits for them, and re-layouts  4.4 us

profile of v5, /device:TPU:33, one launch (start us, length us, event | category | flops | bytes accessed | tf_op | source)
XLA Modules:
  0.0 183.4 jit_solution(9255178075009449030)
XLA Ops:
  0.0 1.4 copy.5.table
  1.4 179.0 %window.1 = bf16[2,1024,512]{2,1,0:T(8,128)(2,1)} custom-call(s32[16,3]{1,0:T(8,128)} %copy.5.table, f32[16]{0:T(128)} %occ.1, bf16[2,1024,512]{2,1,0:T(8,128)(2,1)} %factors.1, f32[16,512]{1,0:T(8,128)} %virt.1), custom_call_target="tpu_custom_call" | custom-call | tf_op jit(solution)/shard_map/window/pallas_call | solution.py:454
  180.4 3.0 %copy.7 = bf16[2,1024,512]{2,1,0:T(8,128)(2,1)} copy(bf16[2,1024,512]{2,1,0:T(8,128)(2,1)} %window.1) | data formatting | bytes 4194304
